TPU v7x, 256 devices: a whole 4x4x8 slice. The times are simulated.
256 devices in a mesh: seq: 64 (over z, x, core), tp: 4 (over y).
Axes of the slice: x: 4, y: 4, z: 8, core: 2. Of those that a mesh axis runs over, the one named last changes fastest.
Arguments:
- tokens: bfloat16 [32768, 2048], P('seq', 'tp'), may hold values from -6 to 6
- norm_gain: float32 [2048], replicated, may hold values from 0.1 to 1.9
- w_query: bfloat16 [2048, 2048], P(None, 'tp'), may hold values from -0.125 to 0.125
- w_keyval: bfloat16 [2048, 256], replicated, may hold values from -0.125 to 0.125
- w_out: bfloat16 [2048, 2048], P('tp'), may hold values from -0.5 to 0.5
- span_lens: int32 [64], P('seq'), may hold values from 1 to 512, 24576 in all
- cached_lens: int32 [64], P('seq'), may hold values from 1 to 1536, 49152 in all
- old_table: int32 [64, 64], P('seq'), may hold values from 0 to 63, each once within a row
- new_table: int32 [64, 64], P('seq'), may hold values from 0 to 63, each once within a row
- old_cache: bfloat16 [4096, 32, 256], P('seq', 'tp'), may hold values from -720 to 720
Outputs:
- mixed: bfloat16 [32768, 2048], P('seq', 'tp')
- new_cache: bfloat16 [4096, 32, 256], P('seq', 'tp')
Inputs may be any that keep to these rules, and one draw needn't show every extreme that they name: Request r's new tokens are the first span_lens[r] of its 512 rows. `old_table`: each row names every device once: each device holds exactly one block of every request. `new_table`: each row names every device once: each device receives exactly one block of every request.
All inputs are finite; a program needn't handle non-finite values. No bound on the sum of `span_lens` or of `cached_lens` on one device may be relied on, other than what follows from the above.
Results may differ from a plain program's by a relative error of at most 0.012.
The roundings to bfloat16 on the way count: a program that leaves them out, or rounds other values in their place, can miss the bound.
Values may be sent and summed in bfloat16 or wider, within the bound.
A program may use at most 128 MiB of HBM per device.

v0:
```python
import jax
import jax.numpy as jnp
from jax import lax
from jax.sharding import PartitionSpec as P

EPSILON = 1e-05
MASKED = -1e30


def normalize(rows, norm_gain):
    values = rows.astype(jnp.float32)
    average = jnp.mean(values, axis=1, keepdims=True)
    centred = values - average
    spread = jnp.mean(centred * centred, axis=1, keepdims=True)
    return (centred * lax.rsqrt(spread + EPSILON) * norm_gain).astype(jnp.bfloat16)


def body(
    tokens,
    norm_gain,
    w_query,
    w_keyval,
    w_out,
    span_lens,
    cached_lens,
    old_table,
    new_table,
    old_cache,
):
    groups = lax.axis_size("seq")
    tp_count = lax.axis_size("tp")
    tp_index = lax.axis_index("tp")
    holders = old_table[0]
    held_len = cached_lens[0]
    span_len = span_lens[0]
    tok_rows = tokens.shape[0]
    share = old_cache.shape[1]
    width = old_cache.shape[2]
    block_rows = share * tp_count
    capacity = groups * block_rows
    arrived = lax.all_to_all(old_cache, "seq", split_axis=0, concat_axis=0, tiled=True)
    cache_share = jnp.take(arrived, holders, axis=0)
    full_rows = lax.all_gather(tokens, "tp", axis=1, tiled=True)
    normed = normalize(full_rows, norm_gain)
    query = jnp.dot(normed, w_query, preferred_element_type=jnp.float32).astype(jnp.bfloat16)
    keyval = jnp.dot(normed, w_keyval, preferred_element_type=jnp.float32).astype(jnp.bfloat16)
    shifted = lax.dynamic_update_slice(
        jnp.zeros((capacity, width), jnp.bfloat16), keyval, (held_len, jnp.int32(0))
    )
    shifted_share = lax.dynamic_slice_in_dim(
        shifted.reshape(groups, block_rows, width), tp_index * share, share, 1
    )
    share_pos = (
        lax.broadcasted_iota(jnp.int32, (groups, share, 1), 0) * block_rows
        + tp_index * share
        + lax.broadcasted_iota(jnp.int32, (groups, share, 1), 1)
    )
    fresh_share = jnp.where(
        share_pos < held_len,
        cache_share,
        jnp.where(share_pos < held_len + span_len, shifted_share, jnp.zeros_like(shifted_share)),
    )
    targets = new_table[0]
    device_ids = lax.broadcasted_iota(jnp.int32, (groups, groups), 0)
    block_ids = lax.broadcasted_iota(jnp.int32, (groups, groups), 1)
    matches = targets[None, :] == device_ids
    sources = jnp.sum(jnp.where(matches, block_ids, 0), axis=1)
    new_cache = lax.all_to_all(
        jnp.take(fresh_share, sources, axis=0), "seq", split_axis=0, concat_axis=0, tiled=True
    )
    cached = lax.all_gather(cache_share, "tp", axis=1, tiled=True).reshape(capacity, width)
    positions = lax.broadcasted_iota(jnp.int32, (capacity, 1), 0)
    fresh = jnp.where(
        positions < held_len,
        cached,
        jnp.where(positions < held_len + span_len, shifted, jnp.zeros_like(shifted)),
    )
    head_size = width // 2
    keys = fresh[:, :head_size]
    values = fresh[:, head_size:]
    local_heads = query.shape[1] // head_size
    query3 = query.reshape(tok_rows, local_heads, head_size)
    scores = jnp.einsum(
        "thd,kd->htk", query3, keys, preferred_element_type=jnp.float32
    ) * head_size ** (-0.5)
    row_pos = lax.broadcasted_iota(jnp.int32, (tok_rows, 1), 0)
    key_pos = lax.broadcasted_iota(jnp.int32, (1, capacity), 1)
    allowed = key_pos <= held_len + row_pos
    scores = jnp.where(allowed[None], scores, MASKED)
    top = jnp.max(scores, axis=2, keepdims=True)
    weights = jnp.exp(scores - top)
    probs = (weights / jnp.sum(weights, axis=2, keepdims=True)).astype(jnp.bfloat16)
    context = jnp.einsum("htk,kd->thd", probs, values, preferred_element_type=jnp.float32).astype(
        jnp.bfloat16
    )
    context = context.reshape(tok_rows, local_heads * head_size)
    partial_out = jnp.dot(context, w_out, preferred_element_type=jnp.float32)
    summed = lax.psum_scatter(
        partial_out.astype(jnp.bfloat16), "tp", scatter_dimension=1, tiled=True
    ).astype(jnp.float32)
    total = tokens.astype(jnp.float32) + summed
    mixed = jnp.where(row_pos < span_len, total, jnp.zeros_like(total)).astype(jnp.bfloat16)
    return (mixed, new_cache)


def solution(mesh):
    in_specs = (
        P("seq", "tp"),
        P(),
        P(None, "tp"),
        P(),
        P("tp", None),
        P("seq"),
        P("seq"),
        P("seq", None),
        P("seq", None),
        P("seq", "tp", None),
    )
    out_specs = (P("seq", "tp"), P("seq", "tp", None))
    return jax.shard_map(body, mesh=mesh, in_specs=in_specs, out_specs=out_specs, check_vma=False)
```

profile of v0, /device:TPU:1, one launch (start us, length us, event | category | flops | bytes accessed | tf_op | source)
XLA Modules:
  0.0 153.1 jit_solution(9230389170875504754)
XLA Ops:
  7.2 0.0 copy-start
  7.2 0.0 copy-start.5
  7.2 0.0 all-gather.5.cloned.1.call-start
  7.2 0.7 all-gather.5.cloned.1.call-update
  7.9 13.0 %all-to-all-start = ((bf16[64,8,256]{2,1,0:T(8,128)(2,1)}), bf16[64,8,256]{2,1,0:T(8,128)(2,1)S(1)}, u32[]{:S(2)}, u32[]{:S(2)}) async-start(bf16[64,8,256]{2,1,0:T(8,128)(2,1)} %param.21), calls=%async_computation | async-start | bytes 524288 | tf_op jit(solution)/shard_map/all_to_all | solution.py:41
  20.9 0.0 all-gather.3.cloned.1.call-start
  22.3 0.7 compare_select_fusion.1
  23.0 0.7 compare_and_fusion.1
  23.6 0.1 fusion.16
  23.7 10.4 %all-to-all-done = bf16[64,8,256]{2,1,0:T(8,128)(2,1)S(1)} async-done(((bf16[64,8,256]{2,1,0:T(8,128)(2,1)}), bf16[64,8,256]{2,1,0:T(8,128)(2,1)S(1)}, u32[]{:S(2)}, u32[]{:S(2)}) %all-to-all-start) | async-done | bytes 262176 | tf_op jit(solution)/shard_map/all_to_all | solution.py:41
  34.1 1.3 gather_fusion
  35.4 11.7 %all-gather.5.cloned.1.call-done = bf16[512,2048]{1,0:T(8,128)(2,1)} async-done(((bf16[512,512]{1,0:T(8,128)(2,1)}), bf16[512,2048]{1,0:T(8,128)(2,1)}) %all-gather.5.cloned.1.call-update) | async-done | bytes 2097168 | tf_op jit(solution)/shard_map/all_gather | solution.py:43
  47.1 0.0 copy-start.1
  47.1 0.0 copy-start.6
  47.1 2.1 %convert_reduce_fusion = f32[512]{0:T(512)S(1)} fusion(bf16[512,2048]{1,0:T(8,128)(2,1)} %all-gather.5.cloned.1.call-done), kind=kLoop, calls=%fused_computation.12 | loop fusion | flops 2096640 | bytes 2099200 | tf_op jit(solution)/shard_map/reduce_sum | solution.py:12
  49.2 2.3 %fusion.8 = f32[512]{0:T(512)S(1)} fusion(bf16[512,2048]{1,0:T(8,128)(2,1)} %all-gather.5.cloned.1.call-done, f32[512]{0:T(512)S(1)} %broadcast_multiply_fusion), kind=kLoop, calls=%fused_computation.15 | loop fusion | flops 4193792 | bytes 2101248 | tf_op jit(solution)/shard_map/reduce_sum | solution.py:14
  51.5 0.0 copy-done.5
  51.5 0.0 copy-done.1
  51.5 0.7 fusion.10
  52.2 0.0 copy-done.6
  52.3 0.0 copy-start.2
  52.3 0.7 convolution_convert_fusion.2
  53.0 0.6 copy-done.2
  53.6 0.1 broadcast.104
  53.7 1.9 %dynamic_update_slice.3 = bf16[2048,256]{1,0:T(8,128)(2,1)S(1)} dynamic-update-slice(bf16[2048,256]{1,0:T(8,128)(2,1)S(1)} %broadcast.104, bf16[512,256]{1,0:T(8,128)(2,1)S(1)} %convolution_convert_fusion.2, s32[]{:T(128)S(6)} %select_n.39, s32[]{:T(128)} %constant.9.clone.1) | dynamic-update-slice | bytes 524292 | tf_op jit(solution)/shard_map/dynamic_update_slice | solution.py:47
  55.6 1.9 %select_select_fusion = (bf16[64,8,256]{2,1,0:T(8,128)(2,1)S(1)}, bf16[64,8,256]{2,1,0:T(8,128)(2,1)}) fusion(bf16[64,32,256]{2,1,0:T(8,128)(2,1)S(1)} %bitcast.57, s32[]{:T(128)S(6)} %select_n.44, pred[64,8]{1,0:T(8,128)(4,1)S(1)} %get-tuple-element.6, pred[64,8]{1,0:T(8,128)(4,1)S(1)} %get-tuple-element.5, bf16[64,8,256]{2,1,0:T(8,128)(2,1)} %gather_fusion, ...), kind=kLoop, calls=%fused_computation.29 | loop fusion | flops 393216 | bytes 1049668 | tf_op jit(solution)/shard_map/jit(_where)/select_n | solution.py:58
  57.5 0.0 all-gather.3.cloned.1.call-update
  57.5 0.2 reduce-scatter.2.cloned.1.call-start
  57.8 1.8 %iota_compare_fusion = pred[512,2048]{0,1:T(8,128)(4,1)} fusion(s32[512]{0:T(512)S(1)} %iota_add_fusion.1), kind=kLoop, calls=%fused_computation.18 | loop fusion | flops 1048576 | bytes 1050624 | tf_op jit(solution)/shard_map/le | solution.py:88
  59.6 4.3 %convolution_convert_fusion.1 = bf16[512,512]{0,1:T(8,128)(2,1)} fusion(bf16[512,2048]{1,0:T(8,128)(2,1)} %copy-done.2, bf16[2048,512]{1,0:T(8,128)(2,1)} %param.14), kind=kOutput, calls=%fused_computation.21 | convolution fusion | flops 1074003968 | bytes 4718592 | tf_op jit(solution)/shard_map/dot_general | solution.py:45
  63.9 21.4 %all-gather.3.cloned.1.call-done = bf16[64,32,256]{2,1,0:T(8,128)(2,1)} async-done(((bf16[64,8,256]{2,1,0:T(8,128)(2,1)}), bf16[64,32,256]{2,1,0:T(8,128)(2,1)}) %all-gather.3.cloned.1.call-update) | async-done | bytes 1048592 | tf_op jit(solution)/shard_map/all_gather | solution.py:71
  85.3 3.8 %bitcast_select_fusion.4 = bf16[2048,256]{1,0:T(8,128)(2,1)} fusion(bf16[64,32,256]{2,1,0:T(8,128)(2,1)} %all-gather.3.cloned.1.call-done, bf16[2048,256]{1,0:T(8,128)(2,1)S(1)} %dynamic_update_slice.3, pred[2048]{0:T(1024)(128)(4,1)S(1)} %get-tuple-element.9, pred[2048]{0:T(1024)(128)(4,1)S(1)} %get-tuple-element.10), kind=kLoop, calls=%fused_computation.24 | loop fusion | flops 1048576 | bytes 3149824 | tf_op jit(solution)/shard_map/jit(_where)/select_n | solution.py:73
  89.1 0.0 copy-start.4
  89.1 10.7 %fusion.19 = (f32[4,512]{1,0:T(4,128)S(1)}, f32[4,512,2048]{1,2,0:T(8,128)}) fusion(pred[512,2048]{0,1:T(8,128)(4,1)} %iota_compare_fusion, bf16[512,4,128]{0,2,1:T(8,128)(2,1)} %bitcast.59, bf16[2048,256]{1,0:T(8,128)(2,1)} %bitcast_select_fusion.4), kind=kOutput, calls=%fused_computation.52 | convolution fusion | flops 1090521088 | bytes 18882560 | tf_op jit(solution)/shard_map/sub | solution.py:91
  99.8 0.0 copy-done.4
  99.8 7.0 %fusion.13 = bf16[128,4,512]{2,0,1:T(8,128)(2,1)S(1)} fusion(f32[4,512,2048]{1,2,0:T(8,128)} %get-tuple-element.8, f32[4,512]{1,0:T(4,128)S(1)} %get-tuple-element.7, bf16[2048,256]{1,0:T(8,128)(2,1)S(1)} %copy-done.4), kind=kOutput, calls=%fused_computation.22 | convolution fusion | flops 1082392576 | bytes 17833984 | tf_op jit(solution)/shard_map/htk,kd->thd/dot_general | solution.py:93
  106.8 0.0 copy-start.7
  106.8 0.0 copy-done
  106.9 0.0 copy-start.3
  106.9 2.6 %convolution_convert_fusion = bf16[512,2048]{1,0:T(8,128)(2,1)} fusion(bf16[512,512]{0,1:T(8,128)(2,1)S(1)} %bitcast.60, bf16[512,2048]{1,0:T(8,128)(2,1)S(1)} %copy-done), kind=kOutput, calls=%fused_computation.19 | convolution fusion | flops 1074790400 | bytes 4718592 | tf_op jit(solution)/shard_map/dot_general | solution.py:97
  109.5 0.0 reduce-scatter.2.cloned.1.call-update
  109.5 0.0 copy-done.7
  109.5 0.1 select_reduce_fusion
  109.7 0.6 gather_fusion.1
  110.3 0.8 broadcast_select_fusion
  111.1 11.5 %all-to-all-start.1 = ((bf16[64,8,256]{2,1,0:T(8,128)(2,1)}), bf16[64,8,256]{2,1,0:T(8,128)(2,1)S(1)}, u32[]{:S(2)}, u32[]{:S(2)}) async-start(bf16[64,8,256]{2,1,0:T(8,128)(2,1)} %broadcast_select_fusion), calls=%async_computation.2 | async-start | bytes 524288 | tf_op jit(solution)/shard_map/all_to_all | solution.py:68
  122.7 13.1 %all-to-all-done.1 = bf16[64,8,256]{2,1,0:T(8,128)(2,1)S(1)} async-done(((bf16[64,8,256]{2,1,0:T(8,128)(2,1)}), bf16[64,8,256]{2,1,0:T(8,128)(2,1)S(1)}, u32[]{:S(2)}, u32[]{:S(2)}) %all-to-all-start.1) | async-done | bytes 262176 | tf_op jit(solution)/shard_map/all_to_all | solution.py:68
  135.8 8.0 %reduce-scatter.2.cloned.1.call-done = bf16[512,512]{1,0:T(8,128)(2,1)} async-done(((bf16[512,2048]{1,0:T(8,128)(2,1)}), bf16[512,512]{1,0:T(8,128)(2,1)}) %reduce-scatter.2.cloned.1.call-update) | async-done | bytes 524304 | tf_op jit(solution)/shard_map/reduce_scatter | solution.py:98
  143.8 0.0 copy-done.3
  143.8 2.0 %select_convert_fusion = bf16[512,512]{1,0:T(8,128)(2,1)} fusion(bf16[512,512]{1,0:T(8,128)(2,1)} %reduce-scatter.2.cloned.1.call-done, bf16[512,512]{1,0:T(8,128)(2,1)S(1)} %copy-done.3, pred[512]{0:T(512)(128)(4,1)S(1)} %iota_compare_fusion.4), kind=kLoop, calls=%fused_computation.25 | loop fusion | flops 1310720 | bytes 1573376 | tf_op jit(solution)/shard_map/convert_element_type | solution.py:102
  145.9 0.7 copy.29
  (10 shorter events, 0.1 us)
Async XLA Ops:
  7.2 99.7 %copy-start = (bf16[512,2048]{1,0:T(8,128)(2,1)S(1)}, bf16[512,2048]{1,0:T(8,128)(2,1)}, u32[]{:S(2)}) copy-start(bf16[512,2048]{1,0:T(8,128)(2,1)} %param.16) | copy-start | bytes 6291460
  7.2 44.3 %copy-start.5 = (f32[2048]{0:T(1024)S(1)}, f32[2048]{0:T(1024)}, u32[]{:S(2)}) copy-start(f32[2048]{0:T(1024)} %param.13) | copy-start | bytes 24580
  7.2 39.9 %all-gather.5.cloned.1.call-start = ((), (), s32[]{:S(2)}) async-start(), calls=%async_computation.4 | async-start | bytes 2621440 | tf_op jit(solution)/shard_map/all_gather | solution.py:43
  7.9 26.2 %all-to-all-start = ((bf16[64,8,256]{2,1,0:T(8,128)(2,1)}), bf16[64,8,256]{2,1,0:T(8,128)(2,1)S(1)}, u32[]{:S(2)}, u32[]{:S(2)}) async-start(bf16[64,8,256]{2,1,0:T(8,128)(2,1)} %param.21), calls=%async_computation | async-start | bytes 524288 | tf_op jit(solution)/shard_map/all_to_all | solution.py:41
  20.9 64.3 %all-gather.3.cloned.1.call-start = ((), (), s32[]{:S(2)}) async-start(), calls=%async_computation.3 | async-start | bytes 1310720 | tf_op jit(solution)/shard_map/all_gather | solution.py:71
  47.1 4.4 %copy-start.1 = (bf16[512,2048]{1,0:T(8,128)(2,1)S(1)}, bf16[512,2048]{1,0:T(8,128)(2,1)}, u32[]{:S(2)}) copy-start(bf16[512,2048]{1,0:T(8,128)(2,1)} %all-gather.5.cloned.1.call-done) | copy-start | bytes 6291460
  47.1 5.1 %copy-start.6 = (bf16[2048,256]{1,0:T(8,128)(2,1)S(1)}, bf16[2048,256]{1,0:T(8,128)(2,1)}, u32[]{:S(2)}) copy-start(bf16[2048,256]{1,0:T(8,128)(2,1)} %param.15) | copy-start | bytes 3145732
  52.3 1.3 copy-start.2
  57.5 86.3 %reduce-scatter.2.cloned.1.call-start = ((), (), s32[]{:S(2)}) async-start(), calls=%async_computation.5 | async-start | bytes 2621440 | tf_op jit(solution)/shard_map/reduce_scatter | solution.py:98
  89.1 10.7 %copy-start.4 = (bf16[2048,256]{1,0:T(8,128)(2,1)S(1)}, bf16[2048,256]{1,0:T(8,128)(2,1)}, u32[]{:S(2)}) copy-start(bf16[2048,256]{1,0:T(8,128)(2,1)} %bitcast_select_fusion.4) | copy-start | bytes 3145732
  106.8 2.7 %copy-start.7 = (s32[1,64]{1,0:T(1,128)S(1)}, s32[1,64]{1,0:T(1,128)}, u32[]{:S(2)}) copy-start(s32[1,64]{1,0:T(1,128)} %param.20) | copy-start | bytes 772
  106.9 37.0 %copy-start.3 = (bf16[512,512]{1,0:T(8,128)(2,1)S(1)}, bf16[512,512]{1,0:T(8,128)(2,1)}, u32[]{:S(2)}) copy-start(bf16[512,512]{1,0:T(8,128)(2,1)} %param.12) | copy-start | bytes 1572868
  111.1 24.7 %all-to-all-start.1 = ((bf16[64,8,256]{2,1,0:T(8,128)(2,1)}), bf16[64,8,256]{2,1,0:T(8,128)(2,1)S(1)}, u32[]{:S(2)}, u32[]{:S(2)}) async-start(bf16[64,8,256]{2,1,0:T(8,128)(2,1)} %broadcast_select_fusion), calls=%async_computation.2 | async-start | bytes 524288 | tf_op jit(solution)/shard_map/all_to_all | solution.py:68
Sparse Core Ops, SparseCore 0:
  9.8 37.2 all-gather.4
  57.6 27.5 all-gather.2
  109.6 34.1 reduce-scatter.1
where the time goes:
time: 154 us; the launch traced here: 153 us
  waiting for transfers between devices  65.4 us (42%)
  matrix products  25.4 us (16%)
  starting transfers between devices  24.8 us (16%)
  other arithmetic  17 us (11%)
  between operations  15.3 us (10%)
  local copies, waits for them, and re-layouts  5.21 us (3%)
    all_gather x1, waiting for transfers between devices, body(): lax.all_gather(cache_share, 'tp', axis=1, tiled=True)  21.4 us
    all_to_all x1, waiting for transfers between devices, body(): lax.all_to_all(jnp.take(fresh_share, sources, axis=0), 'seq', split_axis=...  13.1 us
    all_to_all x1, starting transfers between devices, body(): lax.all_to_all(old_cache, 'seq', split_axis=0, concat_axis=0, tiled=True)  13 us
    all_gather x1, waiting for transfers between devices, body(): full_rows = lax.all_gather(tokens, 'tp', axis=1, tiled=True)  11.7 us
    all_to_all x1, starting transfers between devices, body(): lax.all_to_all(jnp.take(fresh_share, sources, axis=0), 'seq', split_axis=...  11.5 us
    sub x1, matrix products, body(): weights = jnp.exp(scores - top)  10.7 us
    all_to_all x1, waiting for transfers between devices, body(): lax.all_to_all(old_cache, 'seq', split_axis=0, concat_axis=0, tiled=True)  10.4 us
    reduce_scatter x1, waiting for transfers between devices, body(): lax.psum_scatter(partial_out.astype(jnp.bfloat16), 'tp', scatter_dimensio...  8.03 us
  transfers between devices with their start and end apart: 5, of which 5 were waited for; matrix products, arithmetic and copies ran while one was open for 7% of the time, Pallas kernels for 0%

commit v1 on v0

--- a/solution.py
+++ b/solution.py
@@ -40,7 +40,16 @@
     capacity = groups * block_rows
     arrived = lax.all_to_all(old_cache, "seq", split_axis=0, concat_axis=0, tiled=True)
     cache_share = jnp.take(arrived, holders, axis=0)
-    full_rows = lax.all_gather(tokens, "tp", axis=1, tiled=True)
+    many = lax.axis_size("tp")
+    tile_out = [(b - 1, b) for b in range(1, many)] + [(many - 1, 0)]
+    now = tokens
+    frames = [now]
+    for _ in [*range(many - 1)]:
+        now = lax.ppermute(now, "tp", tile_out)
+        frames += [now]
+    newest = jnp.concatenate([*reversed(frames)], 1)
+    parts_out = lax.axis_index("tp")
+    full_rows = jnp.roll(newest, (parts_out + 1) * now.shape[1], 1)
     normed = normalize(full_rows, norm_gain)
     query = jnp.dot(normed, w_query, preferred_element_type=jnp.float32).astype(jnp.bfloat16)
     keyval = jnp.dot(normed, w_keyval, preferred_element_type=jnp.float32).astype(jnp.bfloat16)

time: 154 us -> 161 us (1.045)
  starting transfers between devices: 24.8 us -> 30.4 us
  local copies, waits for them, and re-layouts: 5.21 us -> 9.3 us
  other arithmetic: 17 us -> 13.6 us
    ppermute x0 -> x3, waiting for transfers between devices: none -> 14.3 us  [body(): now = lax.ppermute(now, 'tp', tile_out)]
    all_gather x1 -> x0, waiting for transfers between devices: 11.7 us -> none  [body(): full_rows = lax.all_gather(tokens, 'tp', axis=1, tiled=True)]
    ppermute x0 -> x3, starting transfers between devices: none -> 5.13 us  [body(): now = lax.ppermute(now, 'tp', tile_out)]
    unnamed x17 -> x22, local copies, waits for them, and re-layouts: 1.35 us -> 5.39 us
    all_to_all x1, waiting for transfers between devices: 10.4 us -> 8.21 us  [body(): lax.all_to_all(old_cache, 'seq', split_axis=0, concat_axis=0, tiled=True)]
    reduce_sum x1, other arithmetic: 2.09 us -> 0.36 us  [normalize(): average = jnp.mean(values, axis=1, keepdims=True)]
  transfers between devices with their start and end apart: 5 -> 7, of which waited for: 5 -> 6; matrix products, arithmetic and copies ran while one was open for 7% -> 7% of each run, Pallas kernels for 0% -> 0%
where the time goes in v1:
time: 161 us; the launch traced here: 160 us
  waiting for transfers between devices  65.6 us (41%)
  starting transfers between devices  30.4 us (19%)
  matrix products  25.7 us (16%)
  between operations  15.6 us (10%)
  other arithmetic  13.6 us (8%)
  local copies, waits for them, and re-layouts  9.3 us (6%)
    all_gather x1, waiting for transfers between devices, body(): lax.all_gather(cache_share, 'tp', axis=1, tiled=True)  21.8 us
    ppermute x3, waiting for transfers between devices, body(): now = lax.ppermute(now, 'tp', tile_out)  14.3 us
    all_to_all x1, starting transfers between devices, body(): lax.all_to_all(old_cache, 'seq', split_axis=0, concat_axis=0, tiled=True)  13.5 us
    all_to_all x1, waiting for transfers between devices, body(): lax.all_to_all(jnp.take(fresh_share, sources, axis=0), 'seq', split_axis=...  13.1 us
    all_to_all x1, starting transfers between devices, body(): lax.all_to_all(jnp.take(fresh_share, sources, axis=0), 'seq', split_axis=...  11.5 us
    sub x1, matrix products, body(): weights = jnp.exp(scores - top)  10.7 us
    all_to_all x1, waiting for transfers between devices, body(): lax.all_to_all(old_cache, 'seq', split_axis=0, concat_axis=0, tiled=True)  8.21 us
    reduce_scatter x1, waiting for transfers between devices, body(): lax.psum_scatter(partial_out.astype(jnp.bfloat16), 'tp', scatter_dimensio...  8.16 us
  transfers between devices with their start and end apart: 7, of which 6 were waited for; matrix products, arithmetic and copies ran while one was open for 7% of the time, Pallas kernels for 0%

profile of v1, /device:TPU:1, one launch (start us, length us, event | category | flops | bytes accessed | tf_op | source)
XLA Modules:
  0.0 160.3 jit_solution(1397621302581382263)
XLA Ops:
  7.2 0.0 copy-start
  7.2 0.0 copy-start.2
  7.2 2.2 %collective-permute-start = (bf16[512,512]{1,0:T(8,128)(2,1)}, bf16[512,512]{1,0:T(8,128)(2,1)S(1)}, u32[]{:S(2)}, u32[]{:S(2)}) collective-permute-start(bf16[512,512]{1,0:T(8,128)(2,1)} %param.12), channel_id=1, source_target_pairs={{0,1},{1,2},{2,3},{3,0},{4,5},{5,6},{6,7},{7,4},{8,9},{9,10},{10,1... | collective-permute-start | bytes 1572872 | tf_op jit(solution)/shard_map/ppermute | solution.py:48
  9.4 11.3 %collective-permute-done = bf16[512,512]{1,0:T(8,128)(2,1)S(1)} collective-permute-done((bf16[512,512]{1,0:T(8,128)(2,1)}, bf16[512,512]{1,0:T(8,128)(2,1)S(1)}, u32[]{:S(2)}, u32[]{:S(2)}) %collective-permute-start) | collective-permute-done | bytes 524320 | tf_op jit(solution)/shard_map/ppermute | solution.py:48
  20.7 1.6 collective-permute-start.1
  22.2 13.5 %all-to-all-start = ((bf16[64,8,256]{2,1,0:T(8,128)(2,1)}), bf16[64,8,256]{2,1,0:T(8,128)(2,1)S(1)}, u32[]{:S(2)}, u32[]{:S(2)}) async-start(bf16[64,8,256]{2,1,0:T(8,128)(2,1)} %param.21), calls=%async_computation | async-start | bytes 524288 | tf_op jit(solution)/shard_map/all_to_all | solution.py:41
  35.7 0.0 all-gather.2.cloned.1.call-start
  37.1 0.8 select_reduce_fusion
  37.8 0.7 compare_select_fusion
  38.5 0.0 collective-permute-done.1
  38.5 1.4 collective-permute-start.2
  39.9 0.7 compare_and_fusion.1
  40.6 0.1 fusion.16
  40.7 8.2 %all-to-all-done = bf16[64,8,256]{2,1,0:T(8,128)(2,1)S(1)} async-done(((bf16[64,8,256]{2,1,0:T(8,128)(2,1)}), bf16[64,8,256]{2,1,0:T(8,128)(2,1)S(1)}, u32[]{:S(2)}, u32[]{:S(2)}) %all-to-all-start) | async-done | bytes 262176 | tf_op jit(solution)/shard_map/all_to_all | solution.py:41
  48.9 1.3 gather_fusion
  50.2 3.0 %collective-permute-done.2 = bf16[512,512]{1,0:T(8,128)(2,1)} collective-permute-done((bf16[512,512]{1,0:T(8,128)(2,1)}, bf16[512,512]{1,0:T(8,128)(2,1)}, u32[]{:S(2)}, u32[]{:S(2)}) %collective-permute-start.2) | collective-permute-done | bytes 524320 | tf_op jit(solution)/shard_map/ppermute | solution.py:48
  53.2 1.1 constant_dynamic-update-slice_fusion.7
  54.3 1.1 constant_dynamic-update-slice_fusion.6
  55.4 0.1 constant_dynamic-update-slice_fusion.5
  55.5 0.0 copy-done.2
  55.5 0.1 constant_dynamic-update-slice_fusion.4
  55.5 0.0 copy-start.5
  55.5 0.0 copy-start.6
  55.6 1.2 constant_dynamic-update-slice_fusion.3
  56.7 1.1 constant_dynamic-update-slice_fusion.2
  57.8 0.1 constant_dynamic-update-slice_fusion.1
  57.9 0.1 constant_dynamic-update-slice_fusion
  58.0 0.0 copy-start.1
  58.0 0.4 convert_reduce_fusion
  58.4 0.7 fusion.8
  59.0 0.0 copy-done.5
  59.1 0.0 copy-done.6
  59.1 0.8 convolution_convert_fusion.2
  59.9 0.0 copy-done.1
  59.9 0.1 broadcast.105
  60.0 1.9 %dynamic_update_slice.3 = bf16[2048,256]{1,0:T(8,128)(2,1)S(1)} dynamic-update-slice(bf16[2048,256]{1,0:T(8,128)(2,1)S(1)} %broadcast.105, bf16[512,256]{1,0:T(8,128)(2,1)S(1)} %convolution_convert_fusion.2, s32[]{:T(128)S(6)} %select_n.54, s32[]{:T(128)} %constant.21.clone.1) | dynamic-update-slice | bytes 524292 | tf_op jit(solution)/shard_map/dynamic_update_slice | solution.py:56
  61.9 1.9 %select_select_fusion = (bf16[64,8,256]{2,1,0:T(8,128)(2,1)S(1)}, bf16[64,8,256]{2,1,0:T(8,128)(2,1)}) fusion(bf16[64,32,256]{2,1,0:T(8,128)(2,1)S(1)} %bitcast.55, s32[]{:T(128)S(6)} %select_n.59, pred[64,8]{1,0:T(8,128)(4,1)S(1)} %get-tuple-element.6, pred[64,8]{1,0:T(8,128)(4,1)S(1)} %get-tuple-element.5, bf16[64,8,256]{2,1,0:T(8,128)(2,1)} %gather_fusion, ...), kind=kLoop, calls=%fused_computation.29 | loop fusion | flops 393216 | bytes 1049668 | tf_op jit(solution)/shard_map/jit(_where)/select_n | solution.py:67
  63.8 0.0 all-gather.2.cloned.1.call-update
  63.8 0.2 reduce-scatter.2.cloned.1.call-start
  64.1 1.8 %iota_compare_fusion = pred[512,2048]{0,1:T(8,128)(4,1)} fusion(s32[512]{0:T(512)S(1)} %iota_add_fusion.1), kind=kLoop, calls=%fused_computation.18 | loop fusion | flops 1048576 | bytes 1050624 | tf_op jit(solution)/shard_map/le | solution.py:97
  65.9 4.5 %convolution_convert_fusion.1 = bf16[512,512]{0,1:T(8,128)(2,1)} fusion(bf16[2048,512]{1,0:T(8,128)(2,1)} %param.14, f32[2048]{0:T(1024)S(1)} %copy-done.6, f32[512]{0:T(512)S(1)} %add_rsqrt_fusion, f32[512]{0:T(512)S(1)} %broadcast_multiply_fusion, bf16[512,4096]{1,0:T(8,128)(2,1)} %copy-done.1, s32[]{:T(128)S(6)} %select_n.53), kind=kOutput, calls=%fused_computation.21 | convolution fusion | flops 1079246848 | bytes 4730884 | tf_op jit(solution)/shard_map/dot_general | solution.py:54
  70.4 21.8 %all-gather.2.cloned.1.call-done = bf16[64,32,256]{2,1,0:T(8,128)(2,1)} async-done(((bf16[64,8,256]{2,1,0:T(8,128)(2,1)}), bf16[64,32,256]{2,1,0:T(8,128)(2,1)}) %all-gather.2.cloned.1.call-update) | async-done | bytes 1048592 | tf_op jit(solution)/shard_map/all_gather | solution.py:80
  92.1 3.8 %bitcast_select_fusion.4 = bf16[2048,256]{1,0:T(8,128)(2,1)} fusion(bf16[64,32,256]{2,1,0:T(8,128)(2,1)} %all-gather.2.cloned.1.call-done, bf16[2048,256]{1,0:T(8,128)(2,1)S(1)} %dynamic_update_slice.3, pred[2048]{0:T(1024)(128)(4,1)S(1)} %get-tuple-element.11, pred[2048]{0:T(1024)(128)(4,1)S(1)} %get-tuple-element.12), kind=kLoop, calls=%fused_computation.24 | loop fusion | flops 1048576 | bytes 3149824 | tf_op jit(solution)/shard_map/jit(_where)/select_n | solution.py:82
  95.9 0.0 copy-start.4
  95.9 10.7 %fusion.21 = (f32[4,512]{1,0:T(4,128)S(1)}, f32[4,512,2048]{1,2,0:T(8,128)}) fusion(pred[512,2048]{0,1:T(8,128)(4,1)} %iota_compare_fusion, bf16[512,4,128]{0,2,1:T(8,128)(2,1)} %bitcast.57, bf16[2048,256]{1,0:T(8,128)(2,1)} %bitcast_select_fusion.4), kind=kOutput, calls=%fused_computation.60 | convolution fusion | flops 1090521088 | bytes 18882560 | tf_op jit(solution)/shard_map/sub | solution.py:100
  106.7 0.0 copy-done.4
  106.7 7.0 %fusion.13 = bf16[128,4,512]{2,0,1:T(8,128)(2,1)S(1)} fusion(f32[4,512,2048]{1,2,0:T(8,128)} %get-tuple-element.8, f32[4,512]{1,0:T(4,128)S(1)} %get-tuple-element.7, bf16[2048,256]{1,0:T(8,128)(2,1)S(1)} %copy-done.4), kind=kOutput, calls=%fused_computation.22 | convolution fusion | flops 1082392576 | bytes 17833984 | tf_op jit(solution)/shard_map/htk,kd->thd/dot_general | solution.py:102
  113.7 0.0 copy-done
  113.7 0.0 copy-start.3
  113.7 2.6 %convolution_convert_fusion = bf16[512,2048]{1,0:T(8,128)(2,1)} fusion(bf16[512,512]{0,1:T(8,128)(2,1)S(1)} %bitcast.58, bf16[512,2048]{1,0:T(8,128)(2,1)S(1)} %copy-done), kind=kOutput, calls=%fused_computation.19 | convolution fusion | flops 1074790400 | bytes 4718592 | tf_op jit(solution)/shard_map/dot_general | solution.py:106
  116.4 0.0 reduce-scatter.2.cloned.1.call-update
  116.4 0.6 gather_fusion.1
  117.0 0.8 broadcast_select_fusion
  117.9 11.5 %all-to-all-start.1 = ((bf16[64,8,256]{2,1,0:T(8,128)(2,1)}), bf16[64,8,256]{2,1,0:T(8,128)(2,1)S(1)}, u32[]{:S(2)}, u32[]{:S(2)}) async-start(bf16[64,8,256]{2,1,0:T(8,128)(2,1)} %broadcast_select_fusion), calls=%async_computation.2 | async-start | bytes 524288 | tf_op jit(solution)/shard_map/all_to_all | solution.py:77
  129.4 13.1 %all-to-all-done.1 = bf16[64,8,256]{2,1,0:T(8,128)(2,1)S(1)} async-done(((bf16[64,8,256]{2,1,0:T(8,128)(2,1)}), bf16[64,8,256]{2,1,0:T(8,128)(2,1)S(1)}, u32[]{:S(2)}, u32[]{:S(2)}) %all-to-all-start.1) | async-done | bytes 262176 | tf_op jit(solution)/shard_map/all_to_all | solution.py:77
  142.6 8.2 %reduce-scatter.2.cloned.1.call-done = bf16[512,512]{1,0:T(8,128)(2,1)} async-done(((bf16[512,2048]{1,0:T(8,128)(2,1)}), bf16[512,512]{1,0:T(8,128)(2,1)}) %reduce-scatter.2.cloned.1.call-update) | async-done | bytes 524304 | tf_op jit(solution)/shard_map/reduce_scatter | solution.py:107
  150.7 0.0 copy-done.3
  150.7 2.0 %select_convert_fusion = bf16[512,512]{1,0:T(8,128)(2,1)} fusion(bf16[512,512]{1,0:T(8,128)(2,1)} %reduce-scatter.2.cloned.1.call-done, bf16[512,512]{1,0:T(8,128)(2,1)S(1)} %copy-done.3, pred[512]{0:T(512)(128)(4,1)S(1)} %iota_compare_fusion.4), kind=kLoop, calls=%fused_computation.25 | loop fusion | flops 1310720 | bytes 1573376 | tf_op jit(solution)/shard_map/convert_element_type | solution.py:111
  152.7 0.7 copy.36
  (9 shorter events, 0.1 us)
Async XLA Ops:
  7.2 106.5 %copy-start = (bf16[512,2048]{1,0:T(8,128)(2,1)S(1)}, bf16[512,2048]{1,0:T(8,128)(2,1)}, u32[]{:S(2)}) copy-start(bf16[512,2048]{1,0:T(8,128)(2,1)} %param.16) | copy-start | bytes 6291460
  7.2 48.3 %copy-start.2 = (bf16[512,512]{1,0:T(8,128)(2,1)S(1)}, bf16[512,512]{1,0:T(8,128)(2,1)}, u32[]{:S(2)}) copy-start(bf16[512,512]{1,0:T(8,128)(2,1)} %param.12) | copy-start | bytes 1572868
  7.2 13.5 %collective-permute-start = (bf16[512,512]{1,0:T(8,128)(2,1)}, bf16[512,512]{1,0:T(8,128)(2,1)S(1)}, u32[]{:S(2)}, u32[]{:S(2)}) collective-permute-start(bf16[512,512]{1,0:T(8,128)(2,1)} %param.12), channel_id=1, source_target_pairs={{0,1},{1,2},{2,3},{3,0},{4,5},{5,6},{6,7},{7,4},{8,9},{9,10},{10,1... | collective-permute-start | bytes 1572872 | tf_op jit(solution)/shard_map/ppermute | solution.py:48
  20.7 17.9 %collective-permute-start.1 = (bf16[512,512]{1,0:T(8,128)(2,1)S(1)}, bf16[512,512]{1,0:T(8,128)(2,1)}, u32[]{:S(2)}, u32[]{:S(2)}) collective-permute-start(bf16[512,512]{1,0:T(8,128)(2,1)S(1)} %collective-permute-done), channel_id=1, source_target_pairs={{0,1},{1,2},{2,3},{3,0},{4,5},{5,6},{6,7},{7,4},{8,9},{9,10},{10,1... | collective-permute-start | bytes 1572872 | tf_op jit(solution)/shard_map/ppermute | solution.py:48
  22.2 26.7 %all-to-all-start = ((bf16[64,8,256]{2,1,0:T(8,128)(2,1)}), bf16[64,8,256]{2,1,0:T(8,128)(2,1)S(1)}, u32[]{:S(2)}, u32[]{:S(2)}) async-start(bf16[64,8,256]{2,1,0:T(8,128)(2,1)} %param.21), calls=%async_computation | async-start | bytes 524288 | tf_op jit(solution)/shard_map/all_to_all | solution.py:41
  35.7 56.4 %all-gather.2.cloned.1.call-start = ((), (), s32[]{:S(2)}) async-start(), calls=%async_computation.3 | async-start | bytes 1310720 | tf_op jit(solution)/shard_map/all_gather | solution.py:80
  38.5 14.6 %collective-permute-start.2 = (bf16[512,512]{1,0:T(8,128)(2,1)}, bf16[512,512]{1,0:T(8,128)(2,1)}, u32[]{:S(2)}, u32[]{:S(2)}) collective-permute-start(bf16[512,512]{1,0:T(8,128)(2,1)} %collective-permute-done.1), channel_id=1, source_target_pairs={{0,1},{1,2},{2,3},{3,0},{4,5},{5,6},{6,7},{7,4},{8,9},{9,10},{10,1... | collective-permute-start | bytes 1572872 | tf_op jit(solution)/shard_map/ppermute | solution.py:48
  55.5 3.5 %copy-start.5 = (bf16[2048,256]{1,0:T(8,128)(2,1)S(1)}, bf16[2048,256]{1,0:T(8,128)(2,1)}, u32[]{:S(2)}) copy-start(bf16[2048,256]{1,0:T(8,128)(2,1)} %param.15) | copy-start | bytes 3145732
  55.5 3.5 %copy-start.6 = (f32[2048]{0:T(1024)S(1)}, f32[2048]{0:T(1024)}, u32[]{:S(2)}) copy-start(f32[2048]{0:T(1024)} %param.13) | copy-start | bytes 24580
  58.0 1.9 %copy-start.1 = (bf16[512,4096]{1,0:T(8,128)(2,1)}, bf16[512,4096]{1,0:T(8,128)(2,1)S(1)}, u32[]{:S(2)}) copy-start(bf16[512,4096]{1,0:T(8,128)(2,1)S(1)} %constant_dynamic-update-slice_fusion) | copy-start | bytes 12582916
  63.8 86.9 %reduce-scatter.2.cloned.1.call-start = ((), (), s32[]{:S(2)}) async-start(), calls=%async_computation.4 | async-start | bytes 2621440 | tf_op jit(solution)/shard_map/reduce_scatter | solution.py:107
  95.9 10.7 %copy-start.4 = (bf16[2048,256]{1,0:T(8,128)(2,1)S(1)}, bf16[2048,256]{1,0:T(8,128)(2,1)}, u32[]{:S(2)}) copy-start(bf16[2048,256]{1,0:T(8,128)(2,1)} %bitcast_select_fusion.4) | copy-start | bytes 3145732
  113.7 37.0 %copy-start.3 = (bf16[512,512]{1,0:T(8,128)(2,1)S(1)}, bf16[512,512]{1,0:T(8,128)(2,1)}, u32[]{:S(2)}) copy-start(bf16[512,512]{1,0:T(8,128)(2,1)} %param.12) | copy-start | bytes 1572868
  117.9 24.7 %all-to-all-start.1 = ((bf16[64,8,256]{2,1,0:T(8,128)(2,1)}), bf16[64,8,256]{2,1,0:T(8,128)(2,1)S(1)}, u32[]{:S(2)}, u32[]{:S(2)}) async-start(bf16[64,8,256]{2,1,0:T(8,128)(2,1)} %broadcast_select_fusion), calls=%async_computation.2 | async-start | bytes 524288 | tf_op jit(solution)/shard_map/all_to_all | solution.py:77
Sparse Core Ops, SparseCore 0:
  64.0 28.1 all-gather.1
  116.5 34.1 reduce-scatter.1
